TPU v7x, 32 devices: a whole 2x2x4 slice. The times are simulated.
32 devices in a mesh: ab: 2 (over y), cd: 16 (over z, x, core).
Axes of the slice: x: 2, y: 2, z: 4, core: 2. Of those that a mesh axis runs over, the one named last changes fastest.
Arguments:
- amplitudes: float32 [768, 16384], P('cd', 'ab'), may hold values from -1.25 to 1.25
- driver: float32 [768, 16384], P('cd', 'ab'), may hold values from -6 to 6
- ladder: bfloat16 [16384, 16384], P('ab', 'cd'), may hold values from -0.125 to 0.125
- block_mask: int32 [128, 128], P('ab', 'cd'), may hold values 0 or 1
- pair_list: int32 [768], replicated, may hold values from 0 to 1023, as said below
- occ_energy: float32 [32], replicated, may hold values from -2 to -0.5
- virt_energy: float32 [128], replicated, may hold values from 0.5 to 3
Outputs:
- new_amplitudes: float32 [768, 16384], P('cd', 'ab')
Inputs may be any that keep to these rules, and one draw needn't show every extreme that they name: `pair_list`: the entries are distinct occupied pairs i * 32 + j. Rows come in aligned blocks of two: a pair with i != j shares its block with the pair (j, i); pairs with i == j stand two to a block. Pairs 0 and 1023 are always listed.
All inputs are finite; a program needn't handle non-finite values. No bound on the sum of `block_mask` on one device may be relied on, other than what follows from the above.
Results may differ from a plain program's by a relative error of at most 0.008.
Values may be sent and summed in bfloat16 or wider, within the bound.
A program may use at most 128 MiB of HBM per device.

v0:
```python
import jax
import jax.numpy as jnp
from jax import lax
from jax.sharding import PartitionSpec as P

NV = 128
NOCC = 32
BLK = 128
ITERS = 2


def swap_rows(values, diagonal_rows):
    row_count = values.shape[0]
    swapped = jnp.flip(values.reshape(row_count // 2, 2, -1), axis=1).reshape(row_count, -1)
    return jnp.where(diagonal_rows[:, None], values, swapped)


def flip_pairs(tiles, diagonal_rows, tile_width):
    row_count = tiles.shape[0]
    tile_count = tiles.shape[1]
    turned = jnp.swapaxes(tiles.reshape(row_count, tile_count, tile_width, tile_width), 2, 3)
    turned = turned.reshape(row_count, tile_count * tile_width * tile_width)
    return swap_rows(turned, diagonal_rows)


def body(amplitudes, driver, ladder, block_mask, pair_list, occ_energy, virt_energy):
    ab_count = lax.axis_size("ab")
    ab_index = lax.axis_index("ab")
    cd_index = lax.axis_index("cd")
    rows_dev, cols_dev = amplitudes.shape
    out_rows, in_cols = ladder.shape
    tile_width = NV // ab_count
    tile_area = tile_width * tile_width
    weights = ladder.reshape(out_rows // BLK, BLK, in_cols // BLK, BLK)
    weights = (weights * block_mask.astype(jnp.bfloat16)[:, None, :, None]).reshape(
        out_rows, in_cols
    )
    pairs_local = ab_index * cols_dev + jnp.arange(cols_dev, dtype=jnp.int32)
    big_a = pairs_local // (tile_width * NV)
    big_b = pairs_local // tile_area % ab_count
    first = big_a * tile_width + pairs_local // tile_width % tile_width
    second = big_b * tile_width + pairs_local % tile_width
    virt_index = jnp.arange(NV, dtype=jnp.int32)
    picks = (first[:, None] == virt_index).astype(jnp.float32) + (
        second[:, None] == virt_index
    ).astype(jnp.float32)
    col_energy = jnp.dot(picks, virt_energy, precision=lax.Precision.HIGHEST)
    row_pairs = lax.dynamic_slice_in_dim(pair_list, cd_index * rows_dev, rows_dev)
    occ_index = jnp.arange(NOCC, dtype=jnp.int32)
    occ_picks = (row_pairs[:, None] // NOCC == occ_index).astype(jnp.float32)
    occ_picks = occ_picks + (row_pairs[:, None] % NOCC == occ_index).astype(jnp.float32)
    row_energy = jnp.dot(occ_picks, occ_energy, precision=lax.Precision.HIGHEST)
    denominator = col_energy[None, :] - row_energy[:, None]
    local_diagonal = row_pairs // NOCC == row_pairs % NOCC
    turned_weights = jnp.swapaxes(
        weights.reshape(out_rows // tile_area, tile_width, tile_width, in_cols), 1, 2
    )
    turned_weights = turned_weights.reshape(out_rows, in_cols)
    state = amplitudes
    for step in range(ITERS):
        rounded = state.astype(jnp.bfloat16)
        regrouped = lax.all_to_all(rounded, "cd", split_axis=1, concat_axis=0, tiled=True)
        partial_value = lax.dot_general(
            lax.all_gather(regrouped, "ab", axis=1, tiled=True),
            weights,
            (((1,), (1,)), ((), ())),
            preferred_element_type=jnp.float32,
        )
        total = lax.psum_scatter(
            partial_value.astype(jnp.bfloat16), "cd", scatter_dimension=0, tiled=True
        ).astype(jnp.float32)
        tiles = lax.all_to_all(
            total.reshape(rows_dev, ab_count, tile_area).astype(jnp.bfloat16),
            "ab",
            split_axis=1,
            concat_axis=1,
            tiled=True,
        ).astype(jnp.float32)
        symmetric = total + flip_pairs(tiles, local_diagonal, tile_width)
        state = (driver + symmetric) / denominator
    return state


def solution(mesh):
    placed = (P("cd", "ab"), P("cd", "ab"), P("ab", "cd"), P("ab", "cd"), P(), P(), P())
    return jax.shard_map(body, mesh=mesh, in_specs=placed, out_specs=P("cd", "ab"), check_vma=False)
```

profile of v0, /device:TPU:0, one launch (start us, length us, event | category | flops | bytes accessed | tf_op | source)
XLA Modules:
  0.0 568.6 jit_solution(2987417950333544323)
XLA Ops:
  6.5 1.5 convert_element_type.47
  8.0 0.1 copy.77
  8.1 0.0 copy-start.2
  8.1 27.4 %all_to_all.48 = bf16[48,16,512]{2,0,1:T(8,128)(2,1)} all-to-all(bf16[48,16,512]{2,0,1:T(8,128)(2,1)S(1)} %bitcast.59), channel_id=1, replica_groups=mesh['ab'=2,'cd'=16] {'cd'}, dimensions={1} | all-to-all | bytes 1572864 | tf_op jit(solution)/shard_map/all_to_all | solution.py:62
  35.5 0.0 all-gather.3.cloned.1.call-update
  35.6 0.0 reduce-scatter.7.cloned.1.call-start
  35.6 0.1 copy.52
  35.7 26.5 %all-gather.3.cloned.1.call-done = bf16[768,1024]{1,0:T(8,128)(2,1)} async-done(((bf16[768,512]{1,0:T(8,128)(2,1)}), bf16[768,1024]{1,0:T(8,128)(2,1)}) %all-gather.3.cloned.1.call-update) | async-done | bytes 1572880 | tf_op jit(solution)/shard_map/all_gather | solution.py:64
  62.2 6.1 %mul.31 = bf16[64,128,8,128]{3,2,1,0:T(8,128)(2,1)} broadcast(bf16[64,8]{1,0:T(8,128)(2,1)S(1)} %copy.52), dimensions={0,2} | broadcast | bytes 16778240 | tf_op jit(solution)/shard_map/mul | solution.py:35
  68.3 22.4 %fusion = bf16[768,8192]{0,1:T(8,128)(2,1)} fusion(bf16[768,1024]{1,0:T(8,128)(2,1)S(1)} %copy-done.3, bf16[8192,1024]{1,0:T(8,128)(2,1)} %param.9, bf16[1024,8,8,128]{3,2,1,0:T(8,128)(2,1)} %bitcast.51), kind=kOutput, calls=%fused_computation.3 | convolution fusion | flops 12899581952 | bytes 47710208 | tf_op jit(solution)/shard_map/dot_general | solution.py:63
  90.7 16.7 %copy.64 = bf16[768,8192]{1,0:T(8,128)(2,1)} copy(bf16[768,8192]{0,1:T(8,128)(2,1)} %fusion) | data formatting | bytes 25165824
  107.4 0.0 reduce-scatter.7.cloned.1.call-update
  107.4 0.1 fusion.10
  107.5 135.0 %reduce-scatter.7.cloned.1.call-done = bf16[48,8192]{1,0:T(8,128)(2,1)} async-done(((bf16[768,8192]{1,0:T(8,128)(2,1)}), bf16[48,8192]{1,0:T(8,128)(2,1)}) %reduce-scatter.7.cloned.1.call-update) | async-done | bytes 786448 | tf_op jit(solution)/shard_map/reduce_scatter | solution.py:69
  242.5 2.0 copy.65
  244.4 0.0 copy-start.4
  244.5 1.6 copy.55
  246.0 3.5 all-to-all-start.1
  249.6 0.0 all-gather.5.cloned.1.call-start
  249.6 0.8 fusion.29
  250.4 0.2 convolution_bitcast_fusion
  250.6 6.4 %fusion.1 = f32[1,8192]{1,0:T(1,128)S(1)} fusion(s32[8192]{0:T(1024)S(1)} %get-tuple-element.9, s32[8192]{0:T(1024)S(1)} %get-tuple-element.8, f32[128]{0:T(128)S(1)} %copy-done), kind=kOutput, calls=%fused_computation.4 | convolution fusion | flops 17825792 | bytes 98816 | tf_op jit(solution)/shard_map/dot_general | solution.py:47
  257.0 2.8 all-to-all-done.1
  259.8 2.4 reshape.147
  262.2 2.4 copy.56
  264.6 1.9 reshape.142
  266.5 2.5 reshape_reshape.6
  269.0 26.0 %rev.7 = f32[24,2,8192]{2,1,0:T(2,128)S(1)} reverse(f32[24,2,8192]{2,1,0:T(2,128)} %reshape_reshape.6), dimensions={1} | reverse | bytes 3145728 | tf_op jit(solution)/shard_map/jit(_flip)/rev | solution.py:14
  295.0 1.1 reshape.143
  296.1 2.7 fusion.7
  298.8 0.1 copy.76
  298.9 25.1 %all_to_all.49 = bf16[48,16,512]{2,0,1:T(8,128)(2,1)} all-to-all(bf16[48,16,512]{2,0,1:T(8,128)(2,1)S(1)} %bitcast.60), channel_id=1, replica_groups=mesh['ab'=2,'cd'=16] {'cd'}, dimensions={1} | all-to-all | bytes 1572864 | tf_op jit(solution)/shard_map/all_to_all | solution.py:62
  324.0 0.0 all-gather.5.cloned.1.call-update
  324.0 0.0 reduce-scatter.9.cloned.1.call-start
  324.1 25.6 %all-gather.5.cloned.1.call-done = bf16[768,1024]{1,0:T(8,128)(2,1)} async-done(((bf16[768,512]{1,0:T(8,128)(2,1)}), bf16[768,1024]{1,0:T(8,128)(2,1)}) %all-gather.5.cloned.1.call-update) | async-done | bytes 1572880 | tf_op jit(solution)/shard_map/all_gather | solution.py:64
  349.7 21.7 %convolution_convert_fusion = bf16[768,8192]{1,0:T(8,128)(2,1)} fusion(bf16[768,1024]{1,0:T(8,128)(2,1)} %all-gather.5.cloned.1.call-done, bf16[8192,1024]{1,0:T(8,128)(2,1)} %param.9, bf16[1024,8,8,128]{3,2,1,0:T(8,128)(2,1)} %bitcast.52), kind=kOutput, calls=%fused_computation.1 | convolution fusion | flops 12899581952 | bytes 47710208 | tf_op jit(solution)/shard_map/dot_general | solution.py:63
  371.4 0.0 reduce-scatter.9.cloned.1.call-update
  371.5 135.0 %reduce-scatter.9.cloned.1.call-done = bf16[48,8192]{1,0:T(8,128)(2,1)} async-done(((bf16[768,8192]{1,0:T(8,128)(2,1)}), bf16[48,8192]{1,0:T(8,128)(2,1)}) %reduce-scatter.9.cloned.1.call-update) | async-done | bytes 786448 | tf_op jit(solution)/shard_map/reduce_scatter | solution.py:69
  506.5 2.0 copy.67
  508.5 0.8 copy.61
  509.3 12.7 %all_to_all.50 = bf16[48,2,4096]{2,0,1:T(8,128)(2,1)S(1)} all-to-all(bf16[48,2,4096]{2,0,1:T(8,128)(2,1)S(1)} %copy.61), channel_id=1, replica_groups=mesh['ab'=2,'cd'=16] {'ab'}, dimensions={1} | all-to-all | bytes 1572864 | tf_op jit(solution)/shard_map/all_to_all | solution.py:72
  522.0 2.4 reshape.148
  524.4 2.4 copy.62
  526.8 1.9 reshape.145
  528.7 2.5 reshape_reshape.7
  531.2 26.0 %rev.8 = f32[24,2,8192]{2,1,0:T(2,128)S(1)} reverse(f32[24,2,8192]{2,1,0:T(2,128)} %reshape_reshape.7), dimensions={1} | reverse | bytes 3145728 | tf_op jit(solution)/shard_map/jit(_flip)/rev | solution.py:14
  557.2 1.1 reshape.146
  558.3 3.8 subtract_divide_fusion
  (10 shorter events, 0.0 us)
Async XLA Ops:
  6.5 244.1 %copy-start = (f32[128]{0:T(128)S(1)}, f32[128]{0:T(128)}, u32[]{:S(2)}) copy-start(f32[128]{0:T(128)} %param.13) | copy-start | bytes 1540
  6.5 55.7 %all-gather.3.cloned.1.call-start = ((), (), s32[]{:S(2)}) async-start(), calls=%async_computation.6 | async-start | bytes 2359296 | tf_op jit(solution)/shard_map/all_gather | solution.py:64
  8.1 27.5 %copy-start.2 = (s32[64,8]{0,1:T(8,128)S(1)}, s32[64,8]{0,1:T(8,128)}, u32[]{:S(2)}) copy-start(s32[64,8]{0,1:T(8,128)} %param.10) | copy-start | bytes 6148
  35.6 206.9 %reduce-scatter.7.cloned.1.call-start = ((), (), s32[]{:S(2)}) async-start(), calls=%async_computation.8 | async-start | bytes 13369344 | tf_op jit(solution)/shard_map/reduce_scatter | solution.py:69
  62.2 6.1 %copy-start.3 = (bf16[768,1024]{1,0:T(8,128)(2,1)S(1)}, bf16[768,1024]{1,0:T(8,128)(2,1)}, u32[]{:S(2)}) copy-start(bf16[768,1024]{1,0:T(8,128)(2,1)} %all-gather.3.cloned.1.call-done) | copy-start | bytes 4718596
  244.4 5.9 %copy-start.4 = (f32[32]{0:T(128)S(1)}, f32[32]{0:T(128)}, u32[]{:S(2)}) copy-start(f32[32]{0:T(128)} %param.12) | copy-start | bytes 388
  246.0 13.8 %all-to-all-start.1 = ((bf16[48,2,4096]{2,0,1:T(8,128)(2,1)}), bf16[48,2,4096]{2,0,1:T(8,128)(2,1)S(1)}, u32[]{:S(2)}, u32[]{:S(2)}) async-start(bf16[48,2,4096]{2,0,1:T(8,128)(2,1)} %copy.55), calls=%async_computation.1 | async-start | bytes 1572864 | tf_op jit(solution)/shard_map/all_to_all | solution.py:72
  249.6 100.2 %all-gather.5.cloned.1.call-start = ((), (), s32[]{:S(2)}) async-start(), calls=%async_computation.7 | async-start | bytes 2359296 | tf_op jit(solution)/shard_map/all_gather | solution.py:64
  324.0 182.4 %reduce-scatter.9.cloned.1.call-start = ((), (), s32[]{:S(2)}) async-start(), calls=%async_computation.9 | async-start | bytes 13369344 | tf_op jit(solution)/shard_map/reduce_scatter | solution.py:69
  558.3 3.8 copy-start.1
Sparse Core Ops, SparseCore 0:
  35.7 26.4 all-gather.2
  107.5 134.9 reduce-scatter.6
  324.2 25.5 all-gather.4
  371.6 134.8 reduce-scatter.8
where the time goes:
time: 574 us; the launch traced here: 569 us
  waiting for transfers between devices  325 us (57%)
  local copies, waits for them, and re-layouts  102 us (18%)
  blocking collectives  65.3 us (11%)
  matrix products  50.7 us (9%)
  between operations  13.3 us (2%)
  other arithmetic  8.87 us (2%)
    reduce_scatter x2, waiting for transfers between devices, body(): lax.psum_scatter(partial_value.astype(jnp.bfloat16), 'cd', scatter_dimens...  270 us
    all_to_all x2, blocking collectives, body(): lax.all_to_all(rounded, 'cd', split_axis=1, concat_axis=0, tiled=True)  52.6 us
    all_gather x2, waiting for transfers between devices, body(): lax.all_gather(regrouped, 'ab', axis=1, tiled=True)  52.1 us
    rev x2, local copies, waits for them, and re-layouts, swap_rows(): jnp.flip(values.reshape(row_count // 2, 2, -1), axis=1)  51.9 us
    dot_general x2, matrix products, body(): lax.dot_general(lax.all_gather(regrouped, 'ab', axis=1, tiled=True), weig...  44.1 us
    unnamed x13, local copies, waits for them, and re-layouts  20.6 us
    all_to_all x1, blocking collectives, body(): lax.all_to_all(total.reshape(rows_dev, ab_count, tile_area).astype(jnp.bf...  12.7 us
  transfers between devices with their start and end apart: 5, of which 5 were waited for; matrix products, arithmetic and copies ran while one was open for 1% of the time, Pallas kernels for 0%

commit v1 on v0

--- a/solution.py
+++ b/solution.py
@@ -7,6 +7,12 @@
 NOCC = 32
 BLK = 128
 ITERS = 2
+
+
+def trade_parts(shard, axis, split, join):
+    pieces = jnp.split(shard, lax.axis_size(axis), axis=split)
+    received = lax.all_to_all(jnp.stack(pieces), axis, 0, 0)
+    return jnp.concatenate(received, axis=join)
 
 
 def swap_rows(values, diagonal_rows):
@@ -59,7 +65,7 @@
     state = amplitudes
     for step in range(ITERS):
         rounded = state.astype(jnp.bfloat16)
-        regrouped = lax.all_to_all(rounded, "cd", split_axis=1, concat_axis=0, tiled=True)
+        regrouped = trade_parts(rounded, "cd", 1, 0)
         partial_value = lax.dot_general(
             lax.all_gather(regrouped, "ab", axis=1, tiled=True),
             weights,

time: 574 us -> 553 us (0.963)
  local copies, waits for them, and re-layouts: 102 us -> 82.1 us
    unnamed x13 -> x40, local copies, waits for them, and re-layouts: 20.6 us -> 0.2 us
where the time goes in v1:
time: 553 us; the launch traced here: 548 us
  waiting for transfers between devices  325 us (59%)
  local copies, waits for them, and re-layouts  82.1 us (15%)
  blocking collectives  65.1 us (12%)
  matrix products  49.6 us (9%)
  between operations  13.5 us (2%)
  other arithmetic  8.87 us (2%)
    reduce_scatter x2, waiting for transfers between devices, body(): lax.psum_scatter(partial_value.astype(jnp.bfloat16), 'cd', scatter_dimens...  270 us
    all_to_all x2, blocking collectives, trade_parts(): received = lax.all_to_all(jnp.stack(pieces), axis, 0, 0)  52.4 us
    all_gather x2, waiting for transfers between devices, body(): lax.all_gather(regrouped, 'ab', axis=1, tiled=True)  52 us
    rev x2, local copies, waits for them, and re-layouts, swap_rows(): jnp.flip(values.reshape(row_count // 2, 2, -1), axis=1)  51.9 us
    dot_general x2, matrix products, body(): lax.dot_general(lax.all_gather(regrouped, 'ab', axis=1, tiled=True), weig...  43 us
    all_to_all x1, blocking collectives, body(): lax.all_to_all(total.reshape(rows_dev, ab_count, tile_area).astype(jnp.bf...  12.7 us
  transfers between devices with their start and end apart: 5, of which 5 were waited for; matrix products, arithmetic and copies ran while one was open for 1% of the time, Pallas kernels for 0%

profile of v1, /device:TPU:0, one launch (start us, length us, event | category | flops | bytes accessed | tf_op | source)
XLA Modules:
  0.0 548.0 jit_solution(3819588129436561461)
XLA Ops:
  6.5 0.0 copy-start
  6.5 0.0 all-gather.3.cloned.1.call-start
  6.5 1.5 convert_element_type.43
  8.1 0.0 copy-start.2
  8.3 27.4 %all_to_all.20 = bf16[16,48,512]{2,1,0:T(8,128)(2,1)} all-to-all(bf16[16,48,512]{2,1,0:T(8,128)(2,1)S(1)} %constant_dynamic-update-slice_fusion), channel_id=1, replica_groups=mesh['ab'=2,'cd'=16] {'cd'}, dimensions={0} | all-to-all | bytes 1572864 | tf_op jit(solution)/shard_map/all_to_all | solution.py:14
  35.7 0.0 all-gather.3.cloned.1.call-update
  35.7 0.0 reduce-scatter.3.cloned.1.call-start
  35.8 0.0 copy-done.2
  35.8 0.1 copy.19
  35.9 26.5 %all-gather.3.cloned.1.call-done = bf16[768,1024]{1,0:T(8,128)(2,1)} async-done(((bf16[768,512]{1,0:T(8,128)(2,1)}), bf16[768,1024]{1,0:T(8,128)(2,1)}) %all-gather.3.cloned.1.call-update) | async-done | bytes 1572880 | tf_op jit(solution)/shard_map/all_gather | solution.py:70
  62.4 6.1 %mul.31 = bf16[64,128,8,128]{3,2,1,0:T(8,128)(2,1)} broadcast(bf16[64,8]{1,0:T(8,128)(2,1)S(1)} %copy.19), dimensions={0,2} | broadcast | bytes 16778240 | tf_op jit(solution)/shard_map/mul | solution.py:41
  68.4 0.0 copy-done.3
  68.4 21.3 %convolution_convert_fusion.1 = bf16[768,8192]{1,0:T(8,128)(2,1)} fusion(bf16[768,1024]{1,0:T(8,128)(2,1)S(1)} %copy-done.3, bf16[8192,1024]{1,0:T(8,128)(2,1)} %param.9, bf16[1024,8,8,128]{3,2,1,0:T(8,128)(2,1)} %bitcast.171), kind=kOutput, calls=%fused_computation.2 | convolution fusion | flops 12899581952 | bytes 47710208 | tf_op jit(solution)/shard_map/dot_general | solution.py:69
  89.8 0.0 reduce-scatter.3.cloned.1.call-update
  89.8 0.1 fusion.9
  89.9 135.0 %reduce-scatter.3.cloned.1.call-done = bf16[48,8192]{1,0:T(8,128)(2,1)} async-done(((bf16[768,8192]{1,0:T(8,128)(2,1)}), bf16[48,8192]{1,0:T(8,128)(2,1)}) %reduce-scatter.3.cloned.1.call-update) | async-done | bytes 786448 | tf_op jit(solution)/shard_map/reduce_scatter | solution.py:75
  224.9 2.1 copy.34
  226.9 3.5 all-to-all-start.1
  230.5 0.0 all-gather.5.cloned.1.call-start
  230.5 0.8 fusion.28
  231.3 0.0 copy-done.4
  231.3 0.2 convolution_bitcast_fusion
  231.5 6.4 %fusion = f32[1,8192]{1,0:T(1,128)S(1)} fusion(s32[8192]{0:T(1024)S(1)} %get-tuple-element.9, s32[8192]{0:T(1024)S(1)} %get-tuple-element.8, f32[128]{0:T(128)S(1)} %copy-done), kind=kOutput, calls=%fused_computation.3 | convolution fusion | flops 17825792 | bytes 98816 | tf_op jit(solution)/shard_map/dot_general | solution.py:53
  237.9 2.8 all-to-all-done.1
  240.7 2.4 reshape.149
  243.1 2.4 copy.21
  245.5 2.6 reshape_reshape.6
  248.0 1.9 reshape.143
  249.9 26.0 %rev.7 = f32[24,2,8192]{2,1,0:T(2,128)S(1)} reverse(f32[24,2,8192]{2,1,0:T(2,128)} %reshape_reshape.6), dimensions={1} | reverse | bytes 3145728 | tf_op jit(solution)/shard_map/jit(_flip)/rev | solution.py:20
  275.9 1.1 reshape.144
  277.0 2.7 fusion.6
  279.9 25.0 %all_to_all.21 = bf16[16,48,512]{2,1,0:T(8,128)(2,1)} all-to-all(bf16[16,48,512]{2,1,0:T(8,128)(2,1)S(1)} %constant_dynamic-update-slice_fusion.16), channel_id=1, replica_groups=mesh['ab'=2,'cd'=16] {'cd'}, dimensions={0} | all-to-all | bytes 1572864 | tf_op jit(solution)/shard_map/all_to_all | solution.py:14
  304.9 0.0 all-gather.5.cloned.1.call-update
  304.9 0.2 reduce-scatter.5.cloned.1.call-start
  305.1 25.5 %all-gather.5.cloned.1.call-done = bf16[768,1024]{1,0:T(8,128)(2,1)} async-done(((bf16[768,512]{1,0:T(8,128)(2,1)}), bf16[768,1024]{1,0:T(8,128)(2,1)}) %all-gather.5.cloned.1.call-update) | async-done | bytes 1572880 | tf_op jit(solution)/shard_map/all_gather | solution.py:70
  330.6 21.7 %convolution_convert_fusion = bf16[768,8192]{1,0:T(8,128)(2,1)} fusion(bf16[768,1024]{1,0:T(8,128)(2,1)} %all-gather.5.cloned.1.call-done, bf16[8192,1024]{1,0:T(8,128)(2,1)} %param.9, bf16[1024,8,8,128]{3,2,1,0:T(8,128)(2,1)} %bitcast.172), kind=kOutput, calls=%fused_computation.1 | convolution fusion | flops 12899581952 | bytes 47710208 | tf_op jit(solution)/shard_map/dot_general | solution.py:69
  352.3 0.0 reduce-scatter.5.cloned.1.call-update
  352.3 135.1 %reduce-scatter.5.cloned.1.call-done = bf16[48,8192]{1,0:T(8,128)(2,1)} async-done(((bf16[768,8192]{1,0:T(8,128)(2,1)}), bf16[48,8192]{1,0:T(8,128)(2,1)}) %reduce-scatter.5.cloned.1.call-update) | async-done | bytes 786448 | tf_op jit(solution)/shard_map/reduce_scatter | solution.py:75
  487.4 1.2 copy.33
  488.6 12.7 %all_to_all.22 = bf16[48,2,4096]{2,0,1:T(8,128)(2,1)S(1)} all-to-all(bf16[48,2,4096]{2,0,1:T(8,128)(2,1)S(1)} %bitcast.176), channel_id=1, replica_groups=mesh['ab'=2,'cd'=16] {'ab'}, dimensions={1} | all-to-all | bytes 1572864 | tf_op jit(solution)/shard_map/all_to_all | solution.py:78
  501.3 2.4 reshape.150
  503.7 2.4 copy.23
  506.1 2.6 reshape_reshape.7
  508.6 1.9 reshape.147
  510.5 26.0 %rev.8 = f32[24,2,8192]{2,1,0:T(2,128)S(1)} reverse(f32[24,2,8192]{2,1,0:T(2,128)} %reshape_reshape.7), dimensions={1} | reverse | bytes 3145728 | tf_op jit(solution)/shard_map/jit(_flip)/rev | solution.py:20
  536.5 1.1 reshape.148
  537.6 0.0 copy-start.1
  537.6 3.8 subtract_divide_fusion
  (37 shorter events, 0.2 us)
Async XLA Ops:
  6.5 225.0 %copy-start = (f32[128]{0:T(128)S(1)}, f32[128]{0:T(128)}, u32[]{:S(2)}) copy-start(f32[128]{0:T(128)} %param.13) | copy-start | bytes 1540
  6.5 55.8 %all-gather.3.cloned.1.call-start = ((), (), s32[]{:S(2)}) async-start(), calls=%async_computation.6 | async-start | bytes 2359296 | tf_op jit(solution)/shard_map/all_gather | solution.py:70
  8.1 27.6 %copy-start.2 = (s32[64,8]{0,1:T(8,128)S(1)}, s32[64,8]{0,1:T(8,128)}, u32[]{:S(2)}) copy-start(s32[64,8]{0,1:T(8,128)} %param.10) | copy-start | bytes 6148
  35.7 189.2 %reduce-scatter.3.cloned.1.call-start = ((), (), s32[]{:S(2)}) async-start(), calls=%async_computation.7 | async-start | bytes 13369344 | tf_op jit(solution)/shard_map/reduce_scatter | solution.py:75
  62.4 6.1 %copy-start.3 = (bf16[768,1024]{1,0:T(8,128)(2,1)S(1)}, bf16[768,1024]{1,0:T(8,128)(2,1)}, u32[]{:S(2)}) copy-start(bf16[768,1024]{1,0:T(8,128)(2,1)} %all-gather.3.cloned.1.call-done) | copy-start | bytes 4718596
  224.9 6.5 %copy-start.4 = (f32[32]{0:T(128)S(1)}, f32[32]{0:T(128)}, u32[]{:S(2)}) copy-start(f32[32]{0:T(128)} %param.12) | copy-start | bytes 388
  226.9 13.8 %all-to-all-start.1 = ((bf16[48,2,4096]{2,0,1:T(8,128)(2,1)}), bf16[48,2,4096]{2,0,1:T(8,128)(2,1)S(1)}, u32[]{:S(2)}, u32[]{:S(2)}) async-start(bf16[48,2,4096]{2,0,1:T(8,128)(2,1)} %bitcast.168), calls=%async_computation.2 | async-start | bytes 1572864 | tf_op jit(solution)/shard_map/all_to_all | solution.py:78
  230.5 100.1 %all-gather.5.cloned.1.call-start = ((), (), s32[]{:S(2)}) async-start(), calls=%async_computation.8 | async-start | bytes 2359296 | tf_op jit(solution)/shard_map/all_gather | solution.py:70
  304.9 182.5 %reduce-scatter.5.cloned.1.call-start = ((), (), s32[]{:S(2)}) async-start(), calls=%async_computation.9 | async-start | bytes 13369344 | tf_op jit(solution)/shard_map/reduce_scatter | solution.py:75
  537.6 3.8 copy-start.1
Sparse Core Ops, SparseCore 0:
  35.8 26.4 all-gather.2
  89.9 134.9 reduce-scatter.2
  305.0 25.5 all-gather.4
  352.5 134.9 reduce-scatter.4
